TPU v7x, 128 devices: a whole 4x4x4 slice. The times are simulated.
128 devices in a mesh: rep: 8 (over x, core), tm: 16 (over y, z).
Axes of the slice: x: 4, y: 4, z: 4, core: 2. Of those that a mesh axis runs over, the one named last changes fastest.
Arguments:
- frames: bfloat16 [8, 65536, 512], P('rep', 'tm'), may hold values from -20 to 20
- first_weight: bfloat16 [2, 512, 512], replicated, may hold values from -0.1875 to 0.1875
- first_bias: float32 [512], replicated, may hold values from -4 to 4
- second_weight: bfloat16 [2, 512, 256], replicated, may hold values from -0.1875 to 0.1875
Outputs:
- propagated: float32 [8, 65536, 256], P('rep', 'tm')
- residual: float32 [8, 65536, 256], P('rep', 'tm')
All inputs are finite; a program needn't handle non-finite values.
Results may differ from a plain program's by a relative error of at most 0.008.
Values may be sent and summed in bfloat16 or wider, within the bound.
A program may use at most 64 MiB of HBM per device.

v0:
```python
import functools

import jax
import jax.numpy as jnp
from jax import lax
from jax.experimental import pallas as pl
from jax.experimental.pallas import tpu as pltpu
from jax.sharding import PartitionSpec as P

FEAT = 256
D1 = 32
D2 = 256
LAG = 1024
HALF = FEAT // 2
HALO = D1 + D2
SUB = 512

F32 = jnp.float32
BF16 = jnp.bfloat16
HI = lax.Precision.HIGHEST
MESH = pl.DeviceIdType.MESH

ridge_level = 0.001


def dot(a, b, precision=None):
    return jnp.dot(a, b, precision=precision, preferred_element_type=F32)


def dot_nt(a, b, precision=None):
    return lax.dot_general(a, b, (((1,), (1,)), ((), ())), precision=precision, preferred_element_type=F32)


def dot_tn(a, b, precision=None):
    return lax.dot_general(a, b, (((0,), (0,)), ((), ())), precision=precision, preferred_element_type=F32)


def remote(src, dst, send, recv, device):
    return pltpu.make_async_remote_copy(
        src_ref=src, dst_ref=dst, send_sem=send, recv_sem=recv, device_id=device, device_id_type=MESH
    )


def packed(m):
    return jnp.concatenate([m[:HALF, :HALF], m[:HALF, HALF:], m[HALF:, HALF:]], 0)


def unpacked(p):
    a, b, d = p[:HALF], p[HALF : 2 * HALF], p[2 * HALF :]
    return jnp.concatenate([jnp.concatenate([a, b], 1), jnp.concatenate([b.T, d], 1)], 0)


class Chain:
    def __init__(self, refs, where):
        self.part, self.got, self.y_in, self.z_in, self.out, self.send, self.recv = refs
        self.rep, self.reps, self.y, self.ny, self.z, self.nz = where
        self.sent = []

    def copy(self, src, dst, slot, device):
        return remote(src, dst, self.send.at[slot], self.recv.at[slot], device)

    def share(self, src_of, dst, mine, count, base, device_of):
        for d in range(1, count):
            to = lax.rem(mine + d, count)
            c = self.copy(src_of(to), dst.at[mine], base + d, device_of(to))
            c.start()
            self.sent.append(c)

    def arrived(self, dst, mine, count, base, device_of):
        for d in range(1, count):
            source = lax.rem(mine + count - d, count)
            self.copy(dst.at[source], dst.at[source], base + d, device_of(source)).wait_recv()

    def by_rep(self, r):
        return {"rep": r}

    def by_y(self, y):
        return {"tm": y * self.nz + self.z}

    def by_z(self, z):
        return {"tm": self.y * self.nz + z}

    def scatter(self):
        self.got[self.rep] = self.part[self.rep]
        self.share(lambda to: self.part.at[to], self.got, self.rep, self.reps, 0, self.by_rep)

    def over_y(self):
        self.arrived(self.got, self.rep, self.reps, 0, self.by_rep)
        self.y_in[self.y] = sum(self.got[k] for k in range(self.reps))
        self.share(lambda to: self.y_in.at[self.y], self.y_in, self.y, self.ny, 8, self.by_y)

    def over_z(self):
        self.arrived(self.y_in, self.y, self.ny, 8, self.by_y)
        self.z_in[self.z] = sum(self.y_in[k] for k in range(self.ny))
        self.share(lambda to: self.z_in.at[self.z], self.z_in, self.z, self.nz, 12, self.by_z)

    def gather(self):
        self.arrived(self.z_in, self.z, self.nz, 12, self.by_z)
        self.out[self.rep] = sum(self.z_in[k] for k in range(self.nz))
        self.share(lambda to: self.out.at[self.rep], self.out, self.rep, self.reps, 16, self.by_rep)

    def finish(self):
        self.arrived(self.out, self.rep, self.reps, 16, self.by_rep)

    def drain(self):
        for c in self.sent:
            c.wait_send()


def moments_kernel(
    shape,
    frames,
    w1_in,
    bias_in,
    w2_in,
    feat_out,
    inst_out,
    lag_out,
    x,
    h,
    f,
    w1,
    bias,
    w2,
    acc,
    total,
    i_part,
    i_got,
    i_y,
    i_z,
    i_all,
    l_part,
    l_got,
    l_y,
    l_z,
    l_all,
    local,
    halo_s,
    halo_r,
    ahead_s,
    ahead_r,
    i_send,
    i_recv,
    l_send,
    l_recv,
):
    reps, tms, ny, nz = shape
    rows = frames.shape[0]
    rep = lax.axis_index("rep")
    tm = lax.axis_index("tm")
    y, z = lax.div(tm, nz), lax.rem(tm, nz)
    where = (rep, reps, y, ny, z, nz)
    inst = Chain((i_part, i_got, i_y, i_z, i_all, i_send, i_recv), where)
    lag = Chain((l_part, l_got, l_y, l_z, l_all, l_send, l_recv), where)
    has_left, has_right = tm > 0, tm < tms - 1

    quarter = rows // 4
    loads = [
        pltpu.make_async_copy(
            frames.at[pl.ds(k * quarter, quarter)], x.at[pl.ds(HALO + k * quarter, quarter)], local.at[k]
        )
        for k in range(4)
    ]
    weights = [
        pltpu.make_async_copy(w1_in, w1, local.at[4]),
        pltpu.make_async_copy(bias_in, bias, local.at[5]),
        pltpu.make_async_copy(w2_in, w2, local.at[6]),
    ]
    for c in (weights[0], loads[0], weights[1], weights[2], *loads[1:]):
        c.start()

    barrier = pltpu.get_barrier_semaphore()

    def greet(device):
        pl.semaphore_signal(barrier, inc=1, device_id=device, device_id_type=MESH)

    for d in range(1, reps):
        greet({"rep": lax.rem(rep + d, reps)})
    for d in range(1, ny):
        greet({"tm": lax.rem(y + d, ny) * nz + z})
    for d in range(1, nz):
        greet({"tm": y * nz + lax.rem(z + d, nz)})

    @pl.when(has_left)
    def _():
        greet({"tm": tm - 1})

    @pl.when(has_right)
    def _():
        greet({"tm": tm + 1})

    peers = reps + ny + nz - 3 + jnp.minimum(tm, 1) + jnp.minimum(tms - 1 - tm, 1)
    pl.semaphore_wait(barrier, peers)

    halo = remote(frames.at[pl.ds(rows - HALO, HALO)], x.at[pl.ds(0, HALO)], halo_s, halo_r, {"tm": tm + 1})

    @pl.when(has_right)
    def _():
        halo.start()

    @pl.when(jnp.logical_not(has_left))
    def _():
        x[0:HALO, :] = jnp.zeros((HALO, x.shape[1]), BF16)

    @pl.when(jnp.logical_not(has_right))
    def _():
        f[rows : rows + LAG, :] = jnp.zeros((LAG, FEAT), BF16)

    def layer1(start, size, keep=None):
        pre = dot(x[pl.ds(HALO + start, size), :], w1[0]) + dot(x[pl.ds(D2 + start, size), :], w1[1]) + bias[...]
        act = 0.5 * pre * (1.0 + jnp.tanh(0.5 * pre))
        if keep is not None:
            act = act * keep
        h[pl.ds(D2 + start, size), :] = act.astype(BF16)

    def layer2(start, size):
        out = dot(h[pl.ds(D2 + start, size), :], w2[0]) + dot(h[pl.ds(start, size), :], w2[1])
        f[pl.ds(start, size), :] = out.astype(BF16)

    def ahead(k, start, size):
        return remote(
            f.at[pl.ds(start, size)], f.at[pl.ds(rows + start, size)], ahead_s.at[k], ahead_r.at[k], {"tm": tm - 1}
        )

    pieces = [ahead(0, SUB, LAG - SUB), ahead(1, 0, SUB)]

    for c in weights:
        c.wait()
    loads[0].wait()
    layer1(D2, SUB - D2)
    layer1(SUB, SUB)
    layer2(SUB, SUB)

    @pl.when(has_left)
    def _():
        pieces[0].start()

    for c in loads[1:]:
        c.wait()
    layer1(2 * SUB, SUB)

    @pl.loop(3, rows // SUB)
    def _(k):
        start = pl.multiple_of(k * SUB, SUB)
        layer2(pl.multiple_of(start - SUB, SUB), SUB)
        layer1(start, SUB)

    layer2(rows - SUB, SUB)

    @pl.when(has_left)
    def _():
        halo.wait_recv()

    layer1(-D2, D2, jnp.where(has_left, 1.0, 0.0).astype(F32))
    layer1(0, D2)
    layer2(0, SUB)

    @pl.when(has_left)
    def _():
        pieces[1].start()

    f_out = pltpu.make_async_copy(f.at[pl.ds(0, rows)], feat_out.at[pl.ds(0, rows)], local.at[7])
    f_out.start()

    subs, step = rows // SUB, LAG // SUB
    acc[...] = jnp.zeros_like(acc)
    total[...] = jnp.zeros_like(total)

    @pl.loop(0, subs)
    def _(k):
        start = pl.multiple_of(k * SUB, SUB)
        fs = f[pl.ds(start, SUB), :]
        edge = ((tm == 0) & (k < step)) | ((tm == tms - 1) & (k >= subs - step))
        weight = jnp.where(edge, 1.0, 2.0).astype(F32)
        acc[:, :FEAT] += weight * dot_tn(fs, fs)
        total[0:1, :] += weight * jnp.sum(fs.astype(F32), axis=0, keepdims=True)

    g = packed(acc[:, :FEAT])
    own = i_part.shape[1] - 8
    for r in range(reps):
        i_part[r, 0:own] = g[own * r : own * (r + 1)]
        i_part[r, own:] = jnp.zeros((8, HALF), F32)
    i_part[0, own : own + 1] = total[0:1, :HALF]
    i_part[0, own + 1 : own + 2] = total[0:1, HALF:]
    inst.scatter()

    @pl.loop(0, subs - step)
    def _(k):
        start = pl.multiple_of(k * SUB, SUB)
        acc[:, FEAT:] += dot_tn(f[pl.ds(start, SUB), :], f[pl.ds(start + LAG, SUB), :])

    inst.over_y()

    @pl.when(has_right)
    def _():
        pieces[0].wait_recv()
        pieces[1].wait_recv()

    a_out = pltpu.make_async_copy(f.at[pl.ds(rows, LAG)], feat_out.at[pl.ds(rows, LAG)], local.at[8])
    a_out.start()

    for k in range(subs - step, subs):
        acc[:, FEAT:] += dot_tn(f[k * SUB : (k + 1) * SUB, :], f[k * SUB + LAG : (k + 1) * SUB + LAG, :])
    c = acc[:, FEAT:]
    s = packed(c + c.T)
    own = l_part.shape[1]
    for r in range(reps):
        l_part[r] = s[own * r : own * (r + 1)]
    lag.scatter()
    inst.over_z()
    lag.over_y()
    inst.gather()
    lag.over_z()
    inst.finish()
    inst_out[...] = i_all[...]
    lag.gather()
    lag.finish()
    lag_out[...] = l_all[...]

    inst.drain()
    lag.drain()

    @pl.when(has_right)
    def _():
        halo.wait_send()

    @pl.when(has_left)
    def _():
        pieces[0].wait_send()
        pieces[1].wait_send()

    f_out.wait()
    a_out.wait()


def moments(shape, frames, w1, bias, w2):
    reps, tms, ny, nz = shape
    rows, channels = frames.shape
    hid = w1.shape[2]
    pi, pl_rows = 3 * HALF // reps + 8, 3 * HALF // reps

    def chain(p):
        return [
            pltpu.VMEM((reps, p, HALF), F32),
            pltpu.VMEM((reps, p, HALF), F32),
            pltpu.VMEM((ny, p, HALF), F32),
            pltpu.VMEM((nz, p, HALF), F32),
            pltpu.VMEM((reps, p, HALF), F32),
        ]

    hbm = pl.BlockSpec(memory_space=pl.ANY)
    vmem = pl.BlockSpec(memory_space=pltpu.VMEM)
    return pl.pallas_call(
        functools.partial(moments_kernel, shape),
        out_shape=(
            jax.ShapeDtypeStruct((rows + LAG, FEAT), BF16),
            jax.ShapeDtypeStruct((reps, pi, HALF), F32),
            jax.ShapeDtypeStruct((reps, pl_rows, HALF), F32),
        ),
        in_specs=[hbm] * 4,
        out_specs=(hbm, vmem, vmem),
        scratch_shapes=[
            pltpu.VMEM((HALO + rows, channels), BF16),
            pltpu.VMEM((D2 + rows, hid), BF16),
            pltpu.VMEM((rows + LAG, FEAT), BF16),
            pltpu.VMEM(w1.shape, BF16),
            pltpu.VMEM((1, hid), F32),
            pltpu.VMEM(w2.shape, BF16),
            pltpu.VMEM((FEAT, 2 * FEAT), F32),
            pltpu.VMEM((8, FEAT), F32),
            *chain(pi),
            *chain(pl_rows),
            pltpu.SemaphoreType.DMA((9,)),
            pltpu.SemaphoreType.DMA,
            pltpu.SemaphoreType.DMA,
            pltpu.SemaphoreType.DMA((2,)),
            pltpu.SemaphoreType.DMA((2,)),
            pltpu.SemaphoreType.DMA((24,)),
            pltpu.SemaphoreType.DMA((24,)),
            pltpu.SemaphoreType.DMA((24,)),
            pltpu.SemaphoreType.DMA((24,)),
        ],
        compiler_params=pltpu.CompilerParams(
            collective_id=0, has_side_effects=True, vmem_limit_bytes=40 << 20
        ),
        name="moments",
    )(frames, w1, bias, w2)


def factor_block(t_ref, out_ref):
    n = HALF
    sub = lax.broadcasted_iota(jnp.int32, (8, n), 0)
    for j in range(n // 8):
        k0 = 8 * j
        rl = t_ref[k0 : k0 + 8, 0:n]
        rr = t_ref[k0 : k0 + 8, n : 2 * n]
        cols = [jnp.broadcast_to(rl[:, k0 + c : k0 + c + 1], (8, n)) for c in range(8)]
        out = jnp.zeros((8, n), F32)
        for c in range(8):
            is_c = sub == c
            rs = lax.rsqrt(jnp.broadcast_to(cols[c][c : c + 1, :], (8, n)))
            ri = rs * rs
            row_l = jnp.broadcast_to(rl[c : c + 1, :], (8, n))
            row_r = jnp.broadcast_to(rr[c : c + 1, :], (8, n))
            out = jnp.where(is_c, row_r * rs, out)
            row_l = row_l * ri
            row_r = row_r * ri
            mult = cols[c]
            rl = jnp.where(is_c, row_l, rl - mult * row_l)
            rr = jnp.where(is_c, row_r, rr - mult * row_r)
            for e in range(c + 1, 8):
                row_e = jnp.broadcast_to(cols[e][c : c + 1, :], (8, n)) * ri
                cols[e] = jnp.where(is_c, row_e, cols[e] - mult * row_e)
        out_ref[k0 : k0 + 8, :] = out
        zl = [jnp.broadcast_to(rl[c : c + 1, :], (8, n)) for c in range(8)]
        zr = [jnp.broadcast_to(rr[c : c + 1, :], (8, n)) for c in range(8)]
        for i in range(j + 1, n // 8):
            i0 = 8 * i
            sl = t_ref[i0 : i0 + 8, 0:n]
            sr = t_ref[i0 : i0 + 8, n : 2 * n]
            b = [jnp.broadcast_to(sl[:, k0 + c : k0 + c + 1], (8, n)) for c in range(8)]
            for c in range(8):
                sl = sl - b[c] * zl[c]
                sr = sr - b[c] * zr[c]
            t_ref[i0 : i0 + 8, 0:n] = sl
            t_ref[i0 : i0 + 8, n : 2 * n] = sr


def project_kernel(tms, pairs, i_ref, l_ref, f_ref, fa_ref, prop_ref, res_ref, t, inv, l_inv, a, w_ref, offs):
    step = pl.program_id(0)
    steps = pl.num_programs(0)
    n = HALF

    @pl.when(step == 0)
    def _():
        scale = 1.0 / (2.0 * pairs)
        own = i_ref.shape[1] - 8
        sums = jnp.concatenate([i_ref[0, own : own + 1], i_ref[0, own + 1 : own + 2]], 1) * scale
        first = lax.broadcasted_iota(jnp.int32, (8, FEAT), 0) == 0
        mean = jnp.where(first, jnp.broadcast_to(sums, (8, FEAT)), 0.0)
        outer = dot_tn(mean, mean, HI)
        reps = i_ref.shape[0]
        ri = lax.broadcasted_iota(jnp.int32, (FEAT, FEAT), 0)
        ci = lax.broadcasted_iota(jnp.int32, (FEAT, FEAT), 1)
        cov = unpacked(jnp.concatenate([i_ref[r, 0:own] for r in range(reps)], 0)) * scale - outer
        a[...] = cov + jnp.where(ri == ci, ridge_level, 0.0).astype(F32)
        lagged = unpacked(jnp.concatenate([l_ref[r] for r in range(reps)], 0)) * scale - outer
        rh = lax.broadcasted_iota(jnp.int32, (n, n), 0)
        ch = lax.broadcasted_iota(jnp.int32, (n, n), 1)
        eye = jnp.where(rh == ch, 1.0, 0.0).astype(F32)
        t[:, 0:n] = a[0:n, 0:n]
        t[:, n:] = eye

        @pl.loop(0, 2)
        def _(b):
            factor_block(t, l_inv.at[b])

            @pl.when(b == 0)
            def _():
                li = l_inv[0]
                low = dot_nt(a[n:, 0:n], li, HI)
                t[:, 0:n] = a[n:, n:] - dot_nt(low, low, HI)
                t[:, n:] = eye
                inv[n:, 0:n] = dot(low, li, HI)

        inv[0:n, 0:n] = l_inv[0]
        inv[0:n, n:] = jnp.zeros((n, n), F32)
        inv[n:, n:] = l_inv[1]
        inv[n:, 0:n] = -dot(l_inv[1], inv[n:, 0:n], HI)
        w = inv[...]
        koop = dot_nt(dot(w, lagged, HI), w, HI)
        both = jnp.concatenate([w.T, dot(koop, w, HI).T], 1)
        high = both.astype(BF16)
        low = (both - high.astype(F32)).astype(BF16)
        w_ref[0] = high
        w_ref[1] = low
        offs[...] = dot(mean, high.astype(F32) + low.astype(F32), HI)

    wh, gh = w_ref[0, :, :FEAT], w_ref[0, :, FEAT:]
    wl, gl = w_ref[1, :, :FEAT], w_ref[1, :, FEAT:]
    now, later = f_ref[...], fa_ref[...]
    prop = dot(now, gh) + dot(now, gl) - offs[0:1, FEAT:]
    white = dot(later, wh) + dot(later, wl) - offs[0:1, :FEAT]
    prop_ref[...] = prop
    valid = (lax.axis_index("tm") < tms - 1) | (step < steps - LAG // SUB)
    res_ref[...] = jnp.where(valid, white - prop, 0.0)


def project(tms, pairs, inst, lag, feature):
    rows = feature.shape[0] - LAG
    whole = lambda ref: pl.BlockSpec(ref.shape, lambda i: (0,) * len(ref.shape))
    out = jax.ShapeDtypeStruct((rows, FEAT), F32)
    return pl.pallas_call(
        functools.partial(project_kernel, tms, pairs),
        grid=(rows // SUB,),
        out_shape=(out, out),
        in_specs=[
            whole(inst),
            whole(lag),
            pl.BlockSpec((SUB, FEAT), lambda i: (i, 0)),
            pl.BlockSpec((SUB, FEAT), lambda i: (i + LAG // SUB, 0)),
        ],
        out_specs=(pl.BlockSpec((SUB, FEAT), lambda i: (i, 0)), pl.BlockSpec((SUB, FEAT), lambda i: (i, 0))),
        scratch_shapes=[
            pltpu.VMEM((HALF, FEAT), F32),
            pltpu.VMEM((FEAT, FEAT), F32),
            pltpu.VMEM((2, HALF, HALF), F32),
            pltpu.VMEM((FEAT, FEAT), F32),
            pltpu.VMEM((2, FEAT, 2 * FEAT), BF16),
            pltpu.VMEM((8, 2 * FEAT), F32),
        ],
        compiler_params=pltpu.CompilerParams(vmem_limit_bytes=32 << 20),
        name="project",
    )(inst, lag, feature, feature)


def solution(mesh):
    reps, tms = mesh.shape["rep"], mesh.shape["tm"]
    ny = nz = int(round(tms**0.5))

    def on_device(frames, first_weight, first_bias, second_weight):
        block = frames[0]
        rows = block.shape[0]
        pairs = float(reps * (tms * rows - LAG))
        feature, inst, lag = moments(
            (reps, tms, ny, nz), block, first_weight, first_bias.reshape(1, -1), second_weight
        )
        propagated, residual = project(tms, pairs, inst, lag, feature)
        return (propagated[None], residual[None])

    placed = (P("rep", "tm", None), P(), P(), P())
    return jax.shard_map(
        on_device,
        mesh=mesh,
        in_specs=placed,
        out_specs=(P("rep", "tm", None), P("rep", "tm", None)),
        check_vma=False,
    )
```

profile of v0, /device:TPU:1, one launch (start us, length us, event | category | flops | bytes accessed | tf_op | source)
XLA Modules:
  0.0 68.6 jit_solution(8045876444333423803)
XLA Ops:
  0.6 0.0 copy-start
  0.6 2.2 %copy-done = bf16[1,4096,512]{2,1,0:T(8,128)(2,1)S(1)} copy-done((bf16[1,4096,512]{2,1,0:T(8,128)(2,1)S(1)}, bf16[1,4096,512]{2,1,0:T(8,128)(2,1)}, u32[]{:S(2)}) %copy-start) | copy-done | bytes 4194328
  2.8 0.0 copy-start.1
  2.8 1.2 %copy-done.1 = bf16[2,512,512]{2,1,0:T(8,128)(2,1)S(1)} copy-done((bf16[2,512,512]{2,1,0:T(8,128)(2,1)S(1)}, bf16[2,512,512]{2,1,0:T(8,128)(2,1)}, u32[]{:S(2)}) %copy-start.1) | copy-done | bytes 1048600
  4.0 0.0 copy-start.2
  4.0 1.0 %copy-done.2 = bf16[2,512,256]{2,1,0:T(8,128)(2,1)S(1)} copy-done((bf16[2,512,256]{2,1,0:T(8,128)(2,1)S(1)}, bf16[2,512,256]{2,1,0:T(8,128)(2,1)}, u32[]{:S(2)}) %copy-start.2) | copy-done | bytes 524312
  5.1 0.0 copy-start.3
  5.1 0.7 copy-done.3
  5.8 44.4 %moments.1 = (bf16[5120,256]{1,0:T(8,128)(2,1)S(1)}, f32[8,56,128]{2,1,0:T(8,128)S(1)}, f32[8,48,128]{2,1,0:T(8,128)S(1)}) custom-call(bf16[4096,512]{1,0:T(8,128)(2,1)S(1)} %bitcast.4, bf16[2,512,512]{2,1,0:T(8,128)(2,1)S(1)} %copy-done.1, f32[1,512]{1,0:T(1,128)S(1)} %bitcast.5, bf16[2,512,256]{2,1,0:T(8,128)(2,1)S(1)} %copy-done.2), custom_call_target="tpu_custom_call" | custom-call | tf_op jit(solution)/shard_map/moments/pallas_call | solution.py:353
  50.2 18.4 %project.1 = (f32[4096,256]{1,0:T(8,128)}, f32[4096,256]{1,0:T(8,128)}) custom-call(f32[8,56,128]{2,1,0:T(8,128)S(1)} %get-tuple-element.7.i_ref, f32[8,48,128]{2,1,0:T(8,128)S(1)} %get-tuple-element.8.l_ref, bf16[5120,256]{1,0:T(8,128)(2,1)S(1)} %get-tuple-element.9.f_ref.fa_ref, bf16[5120,256]{1,0:T(8,128)(2,1)S(1)} %get-tuple-element.9.f_ref.fa_ref), custom_call_target="tpu_custom_call" | custom-call | tf_op jit(solution)/shard_map/project/pallas_call | solution.py:493
Async XLA Ops:
  0.6 2.2 %copy-start = (bf16[1,4096,512]{2,1,0:T(8,128)(2,1)S(1)}, bf16[1,4096,512]{2,1,0:T(8,128)(2,1)}, u32[]{:S(2)}) copy-start(bf16[1,4096,512]{2,1,0:T(8,128)(2,1)} %param.4) | copy-start | bytes 12582916
  2.8 1.2 %copy-start.1 = (bf16[2,512,512]{2,1,0:T(8,128)(2,1)S(1)}, bf16[2,512,512]{2,1,0:T(8,128)(2,1)}, u32[]{:S(2)}) copy-start(bf16[2,512,512]{2,1,0:T(8,128)(2,1)} %w1_in.1) | copy-start | bytes 3145732
  4.0 1.0 %copy-start.2 = (bf16[2,512,256]{2,1,0:T(8,128)(2,1)S(1)}, bf16[2,512,256]{2,1,0:T(8,128)(2,1)}, u32[]{:S(2)}) copy-start(bf16[2,512,256]{2,1,0:T(8,128)(2,1)} %w2_in.1) | copy-start | bytes 1572868
  5.1 0.7 copy-start.3
where the time goes:
time: 68.8 us; the launch traced here: 68.6 us
  Pallas kernels  62.8 us (91%)
  local copies, waits for them, and re-layouts  5.13 us (7%)
    pallas_call x1, Pallas kernels, moments(): pl.pallas_call(functools.partial(moments_kernel, shape), out_shape=(jax.S...  44.4 us
    pallas_call x1, Pallas kernels, project(): pl.pallas_call(functools.partial(project_kernel, tms, pairs), grid=(rows...  18.4 us
    unnamed x8, local copies, waits for them, and re-layouts  5.13 us

commit v1 on v0

--- a/solution.py
+++ b/solution.py
@@ -41,13 +41,32 @@
     )
 
 
-def packed(m):
-    return jnp.concatenate([m[:HALF, :HALF], m[:HALF, HALF:], m[HALF:, HALF:]], 0)
-
-
-def unpacked(p):
-    a, b, d = p[:HALF], p[HALF : 2 * HALF], p[2 * HALF :]
-    return jnp.concatenate([jnp.concatenate([a, b], 1), jnp.concatenate([b.T, d], 1)], 0)
+def grid_of(n):
+    return lax.broadcasted_iota(jnp.int32, (n, n), 0), lax.broadcasted_iota(jnp.int32, (n, n), 1)
+
+
+def pack(m, part, extra):
+    r, c = grid_of(HALF)
+    low = m[HALF:, HALF:]
+    both = jnp.concatenate([jnp.where(r <= c, m[:HALF, :HALF], low), m[:HALF, HALF:]], 0)
+    own = part.shape[1] - 8
+    for k in range(part.shape[0]):
+        part[k, 0:own] = both[own * k : own * (k + 1)]
+        part[k, own:] = jnp.zeros((8, HALF), F32)
+    part[0, own : own + 1] = jnp.sum(jnp.where(r == c, low, 0.0), axis=0, keepdims=True)
+    for k, row in enumerate(extra):
+        part[0, own + 1 + k : own + 2 + k] = row
+
+
+def unpack(part):
+    r, c = grid_of(HALF)
+    own = part.shape[1] - 8
+    both = jnp.concatenate([part[k, 0:own] for k in range(part.shape[0])], 0)
+    tri, side = both[:HALF], both[HALF:]
+    flip = tri.T
+    high = jnp.where(r <= c, tri, flip)
+    low = jnp.where(r > c, tri, jnp.where(r == c, part[0, own : own + 1], flip))
+    return jnp.concatenate([jnp.concatenate([high, side], 1), jnp.concatenate([side.T, low], 1)], 0)
 
 
 class Chain:
@@ -109,13 +128,14 @@
 
 def moments_kernel(
     shape,
+    pairs,
     frames,
     w1_in,
     bias_in,
     w2_in,
     feat_out,
-    inst_out,
-    lag_out,
+    w_out,
+    offs_out,
     x,
     h,
     f,
@@ -123,7 +143,10 @@
     bias,
     w2,
     acc,
-    total,
+    a,
+    t,
+    inv,
+    l_inv,
     i_part,
     i_got,
     i_y,
@@ -207,15 +230,16 @@
         f[rows : rows + LAG, :] = jnp.zeros((LAG, FEAT), BF16)
 
     def layer1(start, size, keep=None):
-        pre = dot(x[pl.ds(HALO + start, size), :], w1[0]) + dot(x[pl.ds(D2 + start, size), :], w1[1]) + bias[...]
-        act = 0.5 * pre * (1.0 + jnp.tanh(0.5 * pre))
+        taps = jnp.concatenate([x[pl.ds(HALO + start, size), :], x[pl.ds(D2 + start, size), :]], 1)
+        half = 0.5 * (dot(taps, w1[...].reshape(-1, w1.shape[2])) + bias[...])
+        act = half + half * jnp.tanh(half)
         if keep is not None:
             act = act * keep
         h[pl.ds(D2 + start, size), :] = act.astype(BF16)
 
     def layer2(start, size):
-        out = dot(h[pl.ds(D2 + start, size), :], w2[0]) + dot(h[pl.ds(start, size), :], w2[1])
-        f[pl.ds(start, size), :] = out.astype(BF16)
+        taps = jnp.concatenate([h[pl.ds(D2 + start, size), :], h[pl.ds(start, size), :]], 1)
+        f[pl.ds(start, size), :] = dot(taps, w2[...].reshape(-1, FEAT)).astype(BF16)
 
     def ahead(k, start, size):
         return remote(
@@ -237,15 +261,20 @@
 
     for c in loads[1:]:
         c.wait()
-    layer1(2 * SUB, SUB)
-
-    @pl.loop(3, rows // SUB)
-    def _(k):
-        start = pl.multiple_of(k * SUB, SUB)
-        layer2(pl.multiple_of(start - SUB, SUB), SUB)
-        layer1(start, SUB)
-
-    layer2(rows - SUB, SUB)
+    layer1(LAG, rows - LAG)
+    layer2(LAG, rows - LAG)
+
+    blocks = rows // LAG
+
+    def gram(k):
+        edge = tm == (0 if k == 0 else tms - 1) if k in (0, blocks - 1) else False
+        weight = jnp.where(edge, 1.0, 2.0).astype(F32)
+        rows_k = f[k * LAG : (k + 1) * LAG, :]
+        return weight * dot_tn(rows_k, rows_k), weight * jnp.sum(rows_k.astype(F32), axis=0, keepdims=True)
+
+    late = [gram(k) for k in range(1, blocks)]
+    acc[:, :FEAT] = sum(g for g, _ in late)
+    total = sum(v for _, v in late)
 
     @pl.when(has_left)
     def _():
@@ -259,36 +288,18 @@
     def _():
         pieces[1].start()
 
+    first, v = gram(0)
+    total = total + v
+    pack(acc[:, :FEAT] + first, i_part, (total[:, :HALF], total[:, HALF:]))
+    inst.scatter()
+
     f_out = pltpu.make_async_copy(f.at[pl.ds(0, rows)], feat_out.at[pl.ds(0, rows)], local.at[7])
     f_out.start()
 
-    subs, step = rows // SUB, LAG // SUB
-    acc[...] = jnp.zeros_like(acc)
-    total[...] = jnp.zeros_like(total)
-
-    @pl.loop(0, subs)
-    def _(k):
-        start = pl.multiple_of(k * SUB, SUB)
-        fs = f[pl.ds(start, SUB), :]
-        edge = ((tm == 0) & (k < step)) | ((tm == tms - 1) & (k >= subs - step))
-        weight = jnp.where(edge, 1.0, 2.0).astype(F32)
-        acc[:, :FEAT] += weight * dot_tn(fs, fs)
-        total[0:1, :] += weight * jnp.sum(fs.astype(F32), axis=0, keepdims=True)
-
-    g = packed(acc[:, :FEAT])
-    own = i_part.shape[1] - 8
-    for r in range(reps):
-        i_part[r, 0:own] = g[own * r : own * (r + 1)]
-        i_part[r, own:] = jnp.zeros((8, HALF), F32)
-    i_part[0, own : own + 1] = total[0:1, :HALF]
-    i_part[0, own + 1 : own + 2] = total[0:1, HALF:]
-    inst.scatter()
-
-    @pl.loop(0, subs - step)
-    def _(k):
-        start = pl.multiple_of(k * SUB, SUB)
-        acc[:, FEAT:] += dot_tn(f[pl.ds(start, SUB), :], f[pl.ds(start + LAG, SUB), :])
-
+    def lagged(k):
+        return dot_tn(f[k * LAG : (k + 1) * LAG, :], f[(k + 1) * LAG : (k + 2) * LAG, :])
+
+    acc[:, FEAT:] = sum(lagged(k) for k in range(blocks - 1))
     inst.over_y()
 
     @pl.when(has_right)
@@ -298,24 +309,49 @@
 
     a_out = pltpu.make_async_copy(f.at[pl.ds(rows, LAG)], feat_out.at[pl.ds(rows, LAG)], local.at[8])
     a_out.start()
-
-    for k in range(subs - step, subs):
-        acc[:, FEAT:] += dot_tn(f[k * SUB : (k + 1) * SUB, :], f[k * SUB + LAG : (k + 1) * SUB + LAG, :])
-    c = acc[:, FEAT:]
-    s = packed(c + c.T)
-    own = l_part.shape[1]
-    for r in range(reps):
-        l_part[r] = s[own * r : own * (r + 1)]
+    c = acc[:, FEAT:] + lagged(blocks - 1)
+    pack(c + c.T, l_part, ())
     lag.scatter()
     inst.over_z()
     lag.over_y()
     inst.gather()
     lag.over_z()
     inst.finish()
-    inst_out[...] = i_all[...]
+
+    n = HALF
+    scale = 1.0 / (2.0 * pairs)
+    own = i_all.shape[1] - 8
+    sums = jnp.concatenate([i_all[0, own + 1 : own + 2], i_all[0, own + 2 : own + 3]], 1) * scale
+    top = lax.broadcasted_iota(jnp.int32, (8, FEAT), 0) == 0
+    mean = jnp.where(top, jnp.broadcast_to(sums, (8, FEAT)), 0.0)
+    outer = dot_tn(mean, mean, HI)
+    ri, ci = grid_of(FEAT)
+    a[...] = unpack(i_all) * scale - outer + jnp.where(ri == ci, ridge_level, 0.0).astype(F32)
+    rh, ch = grid_of(n)
+    eye = jnp.where(rh == ch, 1.0, 0.0).astype(F32)
+    t[:, 0:n] = a[0:n, 0:n]
+    t[:, n:] = eye
+    factor_block(t, l_inv.at[0])
     lag.gather()
+    li = l_inv[0]
+    low = dot_nt(a[n:, 0:n], li, HI)
+    t[:, 0:n] = a[n:, n:] - dot_nt(low, low, HI)
+    t[:, n:] = eye
+    side = dot(low, li, HI)
+    factor_block(t, l_inv.at[1])
+    inv[0:n, 0:n] = l_inv[0]
+    inv[0:n, n:] = jnp.zeros((n, n), F32)
+    inv[n:, n:] = l_inv[1]
+    inv[n:, 0:n] = -dot(l_inv[1], side, HI)
     lag.finish()
-    lag_out[...] = l_all[...]
+    w = inv[...]
+    koop = dot_nt(dot(w, unpack(l_all) * scale - outer, HI), w, HI)
+    both = jnp.concatenate([w.T, dot(koop, w, HI).T], 1)
+    high = both.astype(BF16)
+    rest = (both - high.astype(F32)).astype(BF16)
+    w_out[0] = high
+    w_out[1] = rest
+    offs_out[...] = dot(mean, high.astype(F32) + rest.astype(F32), HI)
 
     inst.drain()
     lag.drain()
@@ -333,29 +369,22 @@
     a_out.wait()
 
 
-def moments(shape, frames, w1, bias, w2):
+def moments(shape, pairs, frames, w1, bias, w2):
     reps, tms, ny, nz = shape
     rows, channels = frames.shape
     hid = w1.shape[2]
-    pi, pl_rows = 3 * HALF // reps + 8, 3 * HALF // reps
-
-    def chain(p):
-        return [
-            pltpu.VMEM((reps, p, HALF), F32),
-            pltpu.VMEM((reps, p, HALF), F32),
-            pltpu.VMEM((ny, p, HALF), F32),
-            pltpu.VMEM((nz, p, HALF), F32),
-            pltpu.VMEM((reps, p, HALF), F32),
-        ]
+    piece = 2 * HALF // reps + 8
+
+    chain = [pltpu.VMEM((k, piece, HALF), F32) for k in (reps, reps, ny, nz, reps)]
 
     hbm = pl.BlockSpec(memory_space=pl.ANY)
     vmem = pl.BlockSpec(memory_space=pltpu.VMEM)
     return pl.pallas_call(
-        functools.partial(moments_kernel, shape),
+        functools.partial(moments_kernel, shape, pairs),
         out_shape=(
             jax.ShapeDtypeStruct((rows + LAG, FEAT), BF16),
-            jax.ShapeDtypeStruct((reps, pi, HALF), F32),
-            jax.ShapeDtypeStruct((reps, pl_rows, HALF), F32),
+            jax.ShapeDtypeStruct((2, FEAT, 2 * FEAT), BF16),
+            jax.ShapeDtypeStruct((8, 2 * FEAT), F32),
         ),
         in_specs=[hbm] * 4,
         out_specs=(hbm, vmem, vmem),
@@ -367,9 +396,12 @@
             pltpu.VMEM((1, hid), F32),
             pltpu.VMEM(w2.shape, BF16),
             pltpu.VMEM((FEAT, 2 * FEAT), F32),
-            pltpu.VMEM((8, FEAT), F32),
-            *chain(pi),
-            *chain(pl_rows),
+            pltpu.VMEM((FEAT, FEAT), F32),
+            pltpu.VMEM((HALF, FEAT), F32),
+            pltpu.VMEM((FEAT, FEAT), F32),
+            pltpu.VMEM((2, HALF, HALF), F32),
+            *chain,
+            *chain,
             pltpu.SemaphoreType.DMA((9,)),
             pltpu.SemaphoreType.DMA,
             pltpu.SemaphoreType.DMA,
@@ -381,7 +413,7 @@
             pltpu.SemaphoreType.DMA((24,)),
         ],
         compiler_params=pltpu.CompilerParams(
-            collective_id=0, has_side_effects=True, vmem_limit_bytes=40 << 20
+            collective_id=0, has_side_effects=True, vmem_limit_bytes=63 << 20
         ),
         name="moments",
     )(frames, w1, bias, w2)
@@ -426,92 +458,34 @@
             t_ref[i0 : i0 + 8, n : 2 * n] = sr
 
 
-def project_kernel(tms, pairs, i_ref, l_ref, f_ref, fa_ref, prop_ref, res_ref, t, inv, l_inv, a, w_ref, offs):
+def project_kernel(tms, w_ref, offs, f_ref, fa_ref, prop_ref, res_ref):
     step = pl.program_id(0)
-    steps = pl.num_programs(0)
-    n = HALF
-
-    @pl.when(step == 0)
-    def _():
-        scale = 1.0 / (2.0 * pairs)
-        own = i_ref.shape[1] - 8
-        sums = jnp.concatenate([i_ref[0, own : own + 1], i_ref[0, own + 1 : own + 2]], 1) * scale
-        first = lax.broadcasted_iota(jnp.int32, (8, FEAT), 0) == 0
-        mean = jnp.where(first, jnp.broadcast_to(sums, (8, FEAT)), 0.0)
-        outer = dot_tn(mean, mean, HI)
-        reps = i_ref.shape[0]
-        ri = lax.broadcasted_iota(jnp.int32, (FEAT, FEAT), 0)
-        ci = lax.broadcasted_iota(jnp.int32, (FEAT, FEAT), 1)
-        cov = unpacked(jnp.concatenate([i_ref[r, 0:own] for r in range(reps)], 0)) * scale - outer
-        a[...] = cov + jnp.where(ri == ci, ridge_level, 0.0).astype(F32)
-        lagged = unpacked(jnp.concatenate([l_ref[r] for r in range(reps)], 0)) * scale - outer
-        rh = lax.broadcasted_iota(jnp.int32, (n, n), 0)
-        ch = lax.broadcasted_iota(jnp.int32, (n, n), 1)
-        eye = jnp.where(rh == ch, 1.0, 0.0).astype(F32)
-        t[:, 0:n] = a[0:n, 0:n]
-        t[:, n:] = eye
-
-        @pl.loop(0, 2)
-        def _(b):
-            factor_block(t, l_inv.at[b])
-
-            @pl.when(b == 0)
-            def _():
-                li = l_inv[0]
-                low = dot_nt(a[n:, 0:n], li, HI)
-                t[:, 0:n] = a[n:, n:] - dot_nt(low, low, HI)
-                t[:, n:] = eye
-                inv[n:, 0:n] = dot(low, li, HI)
-
-        inv[0:n, 0:n] = l_inv[0]
-        inv[0:n, n:] = jnp.zeros((n, n), F32)
-        inv[n:, n:] = l_inv[1]
-        inv[n:, 0:n] = -dot(l_inv[1], inv[n:, 0:n], HI)
-        w = inv[...]
-        koop = dot_nt(dot(w, lagged, HI), w, HI)
-        both = jnp.concatenate([w.T, dot(koop, w, HI).T], 1)
-        high = both.astype(BF16)
-        low = (both - high.astype(F32)).astype(BF16)
-        w_ref[0] = high
-        w_ref[1] = low
-        offs[...] = dot(mean, high.astype(F32) + low.astype(F32), HI)
-
-    wh, gh = w_ref[0, :, :FEAT], w_ref[0, :, FEAT:]
-    wl, gl = w_ref[1, :, :FEAT], w_ref[1, :, FEAT:]
     now, later = f_ref[...], fa_ref[...]
-    prop = dot(now, gh) + dot(now, gl) - offs[0:1, FEAT:]
-    white = dot(later, wh) + dot(later, wl) - offs[0:1, :FEAT]
+    prop = dot(now, w_ref[0, :, FEAT:]) + dot(now, w_ref[1, :, FEAT:]) - offs[0:1, FEAT:]
+    white = dot(later, w_ref[0, :, :FEAT]) + dot(later, w_ref[1, :, :FEAT]) - offs[0:1, :FEAT]
     prop_ref[...] = prop
-    valid = (lax.axis_index("tm") < tms - 1) | (step < steps - LAG // SUB)
+    valid = (lax.axis_index("tm") < tms - 1) | (step < pl.num_programs(0) - LAG // SUB)
     res_ref[...] = jnp.where(valid, white - prop, 0.0)
 
 
-def project(tms, pairs, inst, lag, feature):
+def project(tms, w, offs, feature):
     rows = feature.shape[0] - LAG
-    whole = lambda ref: pl.BlockSpec(ref.shape, lambda i: (0,) * len(ref.shape))
     out = jax.ShapeDtypeStruct((rows, FEAT), F32)
+    block = pl.BlockSpec((SUB, FEAT), lambda i: (i, 0))
     return pl.pallas_call(
-        functools.partial(project_kernel, tms, pairs),
+        functools.partial(project_kernel, tms),
         grid=(rows // SUB,),
         out_shape=(out, out),
         in_specs=[
-            whole(inst),
-            whole(lag),
-            pl.BlockSpec((SUB, FEAT), lambda i: (i, 0)),
+            pl.BlockSpec(w.shape, lambda i: (0, 0, 0)),
+            pl.BlockSpec(offs.shape, lambda i: (0, 0)),
+            block,
             pl.BlockSpec((SUB, FEAT), lambda i: (i + LAG // SUB, 0)),
         ],
-        out_specs=(pl.BlockSpec((SUB, FEAT), lambda i: (i, 0)), pl.BlockSpec((SUB, FEAT), lambda i: (i, 0))),
-        scratch_shapes=[
-            pltpu.VMEM((HALF, FEAT), F32),
-            pltpu.VMEM((FEAT, FEAT), F32),
-            pltpu.VMEM((2, HALF, HALF), F32),
-            pltpu.VMEM((FEAT, FEAT), F32),
-            pltpu.VMEM((2, FEAT, 2 * FEAT), BF16),
-            pltpu.VMEM((8, 2 * FEAT), F32),
-        ],
-        compiler_params=pltpu.CompilerParams(vmem_limit_bytes=32 << 20),
+        out_specs=(block, block),
+        compiler_params=pltpu.CompilerParams(vmem_limit_bytes=63 << 20),
         name="project",
-    )(inst, lag, feature, feature)
+    )(w, offs, feature, feature)
 
 
 def solution(mesh):
@@ -522,10 +496,10 @@
         block = frames[0]
         rows = block.shape[0]
         pairs = float(reps * (tms * rows - LAG))
-        feature, inst, lag = moments(
-            (reps, tms, ny, nz), block, first_weight, first_bias.reshape(1, -1), second_weight
+        feature, w, offs = moments(
+            (reps, tms, ny, nz), pairs, block, first_weight, first_bias.reshape(1, -1), second_weight
         )
-        propagated, residual = project(tms, pairs, inst, lag, feature)
+        propagated, residual = project(tms, w, offs, feature)
         return (propagated[None], residual[None])
 
     placed = (P("rep", "tm", None), P(), P(), P())

time: 68.8 us -> 63.3 us (0.920)
  local copies, waits for them, and re-layouts: 5.13 us -> 0 us
    unnamed x8 -> x0, local copies, waits for them, and re-layouts: 5.13 us -> none
where the time goes in v1:
time: 63.3 us; the launch traced here: 63 us
  Pallas kernels  62.4 us (99%)
  between operations  0.64 us (1%)
    pallas_call x1, Pallas kernels, moments(): pl.pallas_call(functools.partial(moments_kernel, shape, pairs), out_shape...  53.5 us
    pallas_call x1, Pallas kernels, project(): pl.pallas_call(functools.partial(project_kernel, tms), grid=(rows // SUB,...  8.9 us

profile of v1, /device:TPU:1, one launch (start us, length us, event | category | flops | bytes accessed | tf_op | source)
XLA Modules:
  0.0 63.0 jit_solution(10931857835291476639)
XLA Ops:
  0.6 53.5 %moments.1 = (bf16[5120,256]{1,0:T(8,128)(2,1)}, bf16[2,256,512]{2,1,0:T(8,128)(2,1)}, f32[8,512]{1,0:T(8,128)}) custom-call(bf16[4096,512]{1,0:T(8,128)(2,1)} %bitcast.4, bf16[2,512,512]{2,1,0:T(8,128)(2,1)} %w1_in.1, f32[1,512]{1,0:T(1,128)} %bitcast.5, bf16[2,512,256]{2,1,0:T(8,128)(2,1)} %w2_in.1), custom_call_target="tpu_custom_call" | custom-call | tf_op jit(solution)/shard_map/moments/pallas_call | solution.py:382
  54.2 8.9 %project.1 = (f32[4096,256]{1,0:T(8,128)}, f32[4096,256]{1,0:T(8,128)}) custom-call(bf16[2,256,512]{2,1,0:T(8,128)(2,1)} %get-tuple-element.7.w_ref, f32[8,512]{1,0:T(8,128)} %get-tuple-element.8.offs, bf16[5120,256]{1,0:T(8,128)(2,1)} %get-tuple-element.9.f_ref.fa_ref, bf16[5120,256]{1,0:T(8,128)(2,1)} %get-tuple-element.9.f_ref.fa_ref), custom_call_target="tpu_custom_call" | custom-call | tf_op jit(solution)/shard_map/project/pallas_call | solution.py:475

commit v2 on v1

--- a/solution.py
+++ b/solution.py
@@ -215,11 +215,21 @@
     peers = reps + ny + nz - 3 + jnp.minimum(tm, 1) + jnp.minimum(tms - 1 - tm, 1)
     pl.semaphore_wait(barrier, peers)
 
-    halo = remote(frames.at[pl.ds(rows - HALO, HALO)], x.at[pl.ds(0, HALO)], halo_s, halo_r, {"tm": tm + 1})
+    halos = [
+        remote(
+            frames.at[pl.ds(rows - HALO + start, size)],
+            x.at[pl.ds(start, size)],
+            halo_s.at[k],
+            halo_r.at[k],
+            {"tm": tm + 1},
+        )
+        for k, (start, size) in enumerate(((D2, D1), (0, D2)))
+    ]
 
     @pl.when(has_right)
     def _():
-        halo.start()
+        halos[0].start()
+        halos[1].start()
 
     @pl.when(jnp.logical_not(has_left))
     def _():
@@ -246,7 +256,7 @@
             f.at[pl.ds(start, size)], f.at[pl.ds(rows + start, size)], ahead_s.at[k], ahead_r.at[k], {"tm": tm - 1}
         )
 
-    pieces = [ahead(0, SUB, LAG - SUB), ahead(1, 0, SUB)]
+    pieces = [ahead(0, SUB, LAG - SUB), ahead(1, D2, SUB - D2), ahead(2, 0, D2)]
 
     for c in weights:
         c.wait()
@@ -262,6 +272,18 @@
     for c in loads[1:]:
         c.wait()
     layer1(LAG, rows - LAG)
+
+    @pl.when(has_left)
+    def _():
+        halos[0].wait_recv()
+
+    layer1(0, D2)
+    layer2(D2, SUB - D2)
+
+    @pl.when(has_left)
+    def _():
+        pieces[1].start()
+
     layer2(LAG, rows - LAG)
 
     blocks = rows // LAG
@@ -278,15 +300,14 @@
 
     @pl.when(has_left)
     def _():
-        halo.wait_recv()
+        halos[1].wait_recv()
 
     layer1(-D2, D2, jnp.where(has_left, 1.0, 0.0).astype(F32))
-    layer1(0, D2)
-    layer2(0, SUB)
-
-    @pl.when(has_left)
-    def _():
-        pieces[1].start()
+    layer2(0, D2)
+
+    @pl.when(has_left)
+    def _():
+        pieces[2].start()
 
     first, v = gram(0)
     total = total + v
@@ -304,8 +325,8 @@
 
     @pl.when(has_right)
     def _():
-        pieces[0].wait_recv()
-        pieces[1].wait_recv()
+        for p in pieces:
+            p.wait_recv()
 
     a_out = pltpu.make_async_copy(f.at[pl.ds(rows, LAG)], feat_out.at[pl.ds(rows, LAG)], local.at[8])
     a_out.start()
@@ -331,14 +352,14 @@
     eye = jnp.where(rh == ch, 1.0, 0.0).astype(F32)
     t[:, 0:n] = a[0:n, 0:n]
     t[:, n:] = eye
-    factor_block(t, l_inv.at[0])
+    factor_block(t, l_inv.at[0], {})
     lag.gather()
     li = l_inv[0]
     low = dot_nt(a[n:, 0:n], li, HI)
     t[:, 0:n] = a[n:, n:] - dot_nt(low, low, HI)
     t[:, n:] = eye
     side = dot(low, li, HI)
-    factor_block(t, l_inv.at[1])
+    factor_block(t, l_inv.at[1], {})
     inv[0:n, 0:n] = l_inv[0]
     inv[0:n, n:] = jnp.zeros((n, n), F32)
     inv[n:, n:] = l_inv[1]
@@ -358,12 +379,13 @@
 
     @pl.when(has_right)
     def _():
-        halo.wait_send()
-
-    @pl.when(has_left)
-    def _():
-        pieces[0].wait_send()
-        pieces[1].wait_send()
+        halos[0].wait_send()
+        halos[1].wait_send()
+
+    @pl.when(has_left)
+    def _():
+        for p in pieces:
+            p.wait_send()
 
     f_out.wait()
     a_out.wait()
@@ -403,10 +425,10 @@
             *chain,
             *chain,
             pltpu.SemaphoreType.DMA((9,)),
-            pltpu.SemaphoreType.DMA,
-            pltpu.SemaphoreType.DMA,
             pltpu.SemaphoreType.DMA((2,)),
             pltpu.SemaphoreType.DMA((2,)),
+            pltpu.SemaphoreType.DMA((3,)),
+            pltpu.SemaphoreType.DMA((3,)),
             pltpu.SemaphoreType.DMA((24,)),
             pltpu.SemaphoreType.DMA((24,)),
             pltpu.SemaphoreType.DMA((24,)),
@@ -419,7 +441,7 @@
     )(frames, w1, bias, w2)
 
 
-def factor_block(t_ref, out_ref):
+def factor_block(t_ref, out_ref, between):
     n = HALF
     sub = lax.broadcasted_iota(jnp.int32, (8, n), 0)
     for j in range(n // 8):
@@ -456,36 +478,62 @@
                 sr = sr - b[c] * zr[c]
             t_ref[i0 : i0 + 8, 0:n] = sl
             t_ref[i0 : i0 + 8, n : 2 * n] = sr
-
-
-def project_kernel(tms, w_ref, offs, f_ref, fa_ref, prop_ref, res_ref):
-    step = pl.program_id(0)
-    now, later = f_ref[...], fa_ref[...]
-    prop = dot(now, w_ref[0, :, FEAT:]) + dot(now, w_ref[1, :, FEAT:]) - offs[0:1, FEAT:]
-    white = dot(later, w_ref[0, :, :FEAT]) + dot(later, w_ref[1, :, :FEAT]) - offs[0:1, :FEAT]
-    prop_ref[...] = prop
-    valid = (lax.axis_index("tm") < tms - 1) | (step < pl.num_programs(0) - LAG // SUB)
-    res_ref[...] = jnp.where(valid, white - prop, 0.0)
+        if j in between:
+            between[j]()
+
+
+def project_kernel(tms, w_in, offs_in, f_in, prop_out, res_out, w, offs, f, prop, res, load, store):
+    rows = prop.shape[0]
+    blocks = rows // LAG
+    last = lax.axis_index("tm") == tms - 1
+    loads = [pltpu.make_async_copy(w_in, w, load.at[0]), pltpu.make_async_copy(offs_in, offs, load.at[1])]
+    loads += [
+        pltpu.make_async_copy(f_in.at[pl.ds(k * LAG, LAG)], f.at[pl.ds(k * LAG, LAG)], load.at[2 + k])
+        for k in range(blocks + 1)
+    ]
+    for c in loads:
+        c.start()
+    for c in loads[:3]:
+        c.wait()
+    stores = []
+    for k in range(rows // SUB):
+        at = pl.ds(k * SUB, SUB)
+        if k * SUB % LAG == 0:
+            loads[3 + k * SUB // LAG].wait()
+        now, later = f[at, :], f[k * SUB + LAG : (k + 1) * SUB + LAG, :]
+        ahead = dot(now, w[0, :, FEAT:]) + dot(now, w[1, :, FEAT:]) - offs[0:1, FEAT:]
+        white = dot(later, w[0, :, :FEAT]) + dot(later, w[1, :, :FEAT]) - offs[0:1, :FEAT]
+        prop[at, :] = ahead
+        gap = white - ahead
+        res[at, :] = jnp.where(last, 0.0, gap) if (k + 1) * SUB > rows - LAG else gap
+        for n, (src, dst) in enumerate(((prop, prop_out), (res, res_out))):
+            stores.append(pltpu.make_async_copy(src.at[at], dst.at[at], store.at[n, k]))
+            stores[-1].start()
+    for c in stores:
+        c.wait()
 
 
 def project(tms, w, offs, feature):
     rows = feature.shape[0] - LAG
     out = jax.ShapeDtypeStruct((rows, FEAT), F32)
-    block = pl.BlockSpec((SUB, FEAT), lambda i: (i, 0))
+    hbm = pl.BlockSpec(memory_space=pl.ANY)
     return pl.pallas_call(
         functools.partial(project_kernel, tms),
-        grid=(rows // SUB,),
         out_shape=(out, out),
-        in_specs=[
-            pl.BlockSpec(w.shape, lambda i: (0, 0, 0)),
-            pl.BlockSpec(offs.shape, lambda i: (0, 0)),
-            block,
-            pl.BlockSpec((SUB, FEAT), lambda i: (i + LAG // SUB, 0)),
+        in_specs=[hbm] * 3,
+        out_specs=(hbm, hbm),
+        scratch_shapes=[
+            pltpu.VMEM(w.shape, BF16),
+            pltpu.VMEM(offs.shape, F32),
+            pltpu.VMEM(feature.shape, BF16),
+            pltpu.VMEM((rows, FEAT), F32),
+            pltpu.VMEM((rows, FEAT), F32),
+            pltpu.SemaphoreType.DMA((3 + rows // LAG,)),
+            pltpu.SemaphoreType.DMA((2, rows // SUB)),
         ],
-        out_specs=(block, block),
         compiler_params=pltpu.CompilerParams(vmem_limit_bytes=63 << 20),
         name="project",
-    )(w, offs, feature, feature)
+    )(w, offs, feature)
 
 
 def solution(mesh):

time: 63.3 us -> 60.2 us (0.951)
  Pallas kernels: 62.4 us -> 59.3 us
    pallas_call x1, Pallas kernels: 8.9 us -> 5.44 us  [project(): pl.pallas_call(functools.partial(project_kernel, tms), out_shape=(out, ou...]
where the time goes in v2:
time: 60.2 us; the launch traced here: 60.1 us
  Pallas kernels  59.3 us (99%)
  between operations  0.8 us (1%)
    pallas_call x1, Pallas kernels, moments(): pl.pallas_call(functools.partial(moments_kernel, shape, pairs), out_shape...  53.8 us
    pallas_call x1, Pallas kernels, project(): pl.pallas_call(functools.partial(project_kernel, tms), out_shape=(out, ou...  5.44 us

profile of v2, /device:TPU:1, one launch (start us, length us, event | category | flops | bytes accessed | tf_op | source)
XLA Modules:
  0.0 60.1 jit_solution(372135283217442239)
XLA Ops:
  0.6 53.8 %moments.1 = (bf16[5120,256]{1,0:T(8,128)(2,1)}, bf16[2,256,512]{2,1,0:T(8,128)(2,1)}, f32[8,512]{1,0:T(8,128)}) custom-call(bf16[4096,512]{1,0:T(8,128)(2,1)} %bitcast.4, bf16[2,512,512]{2,1,0:T(8,128)(2,1)} %w1_in.1, f32[1,512]{1,0:T(1,128)} %bitcast.5, bf16[2,512,256]{2,1,0:T(8,128)(2,1)} %w2_in.1), custom_call_target="tpu_custom_call" | custom-call | tf_op jit(solution)/shard_map/moments/pallas_call | solution.py:404
  54.5 5.4 %project.1 = (f32[4096,256]{1,0:T(8,128)}, f32[4096,256]{1,0:T(8,128)}) custom-call(bf16[2,256,512]{2,1,0:T(8,128)(2,1)} %get-tuple-element.7.w_in, f32[8,512]{1,0:T(8,128)} %get-tuple-element.8.offs_in, bf16[5120,256]{1,0:T(8,128)(2,1)} %get-tuple-element.9.f_in), custom_call_target="tpu_custom_call" | custom-call | tf_op jit(solution)/shard_map/project/pallas_call | solution.py:520

commit v3 on v2

--- a/solution.py
+++ b/solution.py
@@ -352,8 +352,7 @@
     eye = jnp.where(rh == ch, 1.0, 0.0).astype(F32)
     t[:, 0:n] = a[0:n, 0:n]
     t[:, n:] = eye
-    factor_block(t, l_inv.at[0], {})
-    lag.gather()
+    factor_block(t, l_inv.at[0], {8: lag.gather})
     li = l_inv[0]
     low = dot_nt(a[n:, 0:n], li, HI)
     t[:, 0:n] = a[n:, n:] - dot_nt(low, low, HI)
@@ -364,10 +363,10 @@
     inv[0:n, n:] = jnp.zeros((n, n), F32)
     inv[n:, n:] = l_inv[1]
     inv[n:, 0:n] = -dot(l_inv[1], side, HI)
+    w = inv[...]
+    wt, gram_w = w.T, dot_tn(w, w, HI)
     lag.finish()
-    w = inv[...]
-    koop = dot_nt(dot(w, unpack(l_all) * scale - outer, HI), w, HI)
-    both = jnp.concatenate([w.T, dot(koop, w, HI).T], 1)
+    both = jnp.concatenate([wt, dot(dot(w, unpack(l_all) * scale - outer, HI), gram_w, HI).T], 1)
     high = both.astype(BF16)
     rest = (both - high.astype(F32)).astype(BF16)
     w_out[0] = high
@@ -441,6 +440,10 @@
     )(frames, w1, bias, w2)
 
 
+def spread(m, c):
+    return jnp.broadcast_to(m[c : c + 1, :], m.shape)
+
+
 def factor_block(t_ref, out_ref, between):
     n = HALF
     sub = lax.broadcasted_iota(jnp.int32, (8, n), 0)
@@ -450,24 +453,27 @@
         rr = t_ref[k0 : k0 + 8, n : 2 * n]
         cols = [jnp.broadcast_to(rl[:, k0 + c : k0 + c + 1], (8, n)) for c in range(8)]
         out = jnp.zeros((8, n), F32)
-        for c in range(8):
-            is_c = sub == c
-            rs = lax.rsqrt(jnp.broadcast_to(cols[c][c : c + 1, :], (8, n)))
-            ri = rs * rs
-            row_l = jnp.broadcast_to(rl[c : c + 1, :], (8, n))
-            row_r = jnp.broadcast_to(rr[c : c + 1, :], (8, n))
-            out = jnp.where(is_c, row_r * rs, out)
-            row_l = row_l * ri
-            row_r = row_r * ri
-            mult = cols[c]
-            rl = jnp.where(is_c, row_l, rl - mult * row_l)
-            rr = jnp.where(is_c, row_r, rr - mult * row_r)
-            for e in range(c + 1, 8):
-                row_e = jnp.broadcast_to(cols[e][c : c + 1, :], (8, n)) * ri
-                cols[e] = jnp.where(is_c, row_e, cols[e] - mult * row_e)
+        for c in range(0, 8, 2):
+            u, v = cols[c], cols[c + 1]
+            p, q, d = spread(u, c), spread(v, c), spread(v, c + 1)
+            rd, rp = lax.rsqrt(p * d - q * q), lax.rsqrt(p)
+            det = rd * rd
+            i11, i12, i22 = d * det, q * det, p * det
+            is0, is1 = sub == c, sub == c + 1
+
+            def solved(m):
+                top, low = spread(m, c), spread(m, c + 1)
+                z0, z1 = i11 * top - i12 * low, i22 * low - i12 * top
+                return top, low, jnp.where(is0, z0, jnp.where(is1, z1, m - u * z0 - v * z1))
+
+            for e in range(c + 2, 8):
+                cols[e] = solved(cols[e])[2]
+            top, low, rr = solved(rr)
+            out = jnp.where(is0, top * rp, jnp.where(is1, low * (rd * p * rp) - top * (rd * q * rp), out))
+            rl = solved(rl)[2]
         out_ref[k0 : k0 + 8, :] = out
-        zl = [jnp.broadcast_to(rl[c : c + 1, :], (8, n)) for c in range(8)]
-        zr = [jnp.broadcast_to(rr[c : c + 1, :], (8, n)) for c in range(8)]
+        zl = [spread(rl, c) for c in range(8)]
+        zr = [spread(rr, c) for c in range(8)]
         for i in range(j + 1, n // 8):
             i0 = 8 * i
             sl = t_ref[i0 : i0 + 8, 0:n]

time: 60.2 us -> 59.4 us (0.987)
  Pallas kernels: 59.3 us -> 58.5 us
    pallas_call x1, Pallas kernels: 53.8 us -> 53.1 us  [moments(): pl.pallas_call(functools.partial(moments_kernel, shape, pairs), out_shape...]
where the time goes in v3:
time: 59.4 us; the launch traced here: 59.3 us
  Pallas kernels  58.5 us (98%)
  between operations  0.8 us (1%)
    pallas_call x1, Pallas kernels, moments(): pl.pallas_call(functools.partial(moments_kernel, shape, pairs), out_shape...  53.1 us
    pallas_call x1, Pallas kernels, project(): pl.pallas_call(functools.partial(project_kernel, tms), out_shape=(out, ou...  5.43 us

profile of v3, /device:TPU:1, one launch (start us, length us, event | category | flops | bytes accessed | tf_op | source)
XLA Modules:
  0.0 59.3 jit_solution(17611290194929897308)
XLA Ops:
  0.6 53.1 %moments.1 = (bf16[5120,256]{1,0:T(8,128)(2,1)}, bf16[2,256,512]{2,1,0:T(8,128)(2,1)}, f32[8,512]{1,0:T(8,128)}) custom-call(bf16[4096,512]{1,0:T(8,128)(2,1)} %bitcast.4, bf16[2,512,512]{2,1,0:T(8,128)(2,1)} %w1_in.1, f32[1,512]{1,0:T(1,128)} %bitcast.5, bf16[2,512,256]{2,1,0:T(8,128)(2,1)} %w2_in.1), custom_call_target="tpu_custom_call" | custom-call | tf_op jit(solution)/shard_map/moments/pallas_call | solution.py:403
  53.7 5.4 %project.1 = (f32[4096,256]{1,0:T(8,128)}, f32[4096,256]{1,0:T(8,128)}) custom-call(bf16[2,256,512]{2,1,0:T(8,128)(2,1)} %get-tuple-element.7.w_in, f32[8,512]{1,0:T(8,128)} %get-tuple-element.8.offs_in, bf16[5120,256]{1,0:T(8,128)(2,1)} %get-tuple-element.9.f_in), custom_call_target="tpu_custom_call" | custom-call | tf_op jit(solution)/shard_map/project/pallas_call | solution.py:526

commit v4 on v3

--- a/solution.py
+++ b/solution.py
@@ -79,7 +79,7 @@
         return remote(src, dst, self.send.at[slot], self.recv.at[slot], device)
 
     def share(self, src_of, dst, mine, count, base, device_of):
-        for d in range(1, count):
+        for d in sorted(range(1, count), key=lambda d: abs(2 * d - count)):
             to = lax.rem(mine + d, count)
             c = self.copy(src_of(to), dst.at[mine], base + d, device_of(to))
             c.start()
@@ -189,9 +189,6 @@
         pltpu.make_async_copy(bias_in, bias, local.at[5]),
         pltpu.make_async_copy(w2_in, w2, local.at[6]),
     ]
-    for c in (weights[0], loads[0], weights[1], weights[2], *loads[1:]):
-        c.start()
-
     barrier = pltpu.get_barrier_semaphore()
 
     def greet(device):
@@ -211,6 +208,9 @@
     @pl.when(has_right)
     def _():
         greet({"tm": tm + 1})
+
+    for c in (weights[0], loads[0], weights[1], weights[2], *loads[1:]):
+        c.start()
 
     peers = reps + ny + nz - 3 + jnp.minimum(tm, 1) + jnp.minimum(tms - 1 - tm, 1)
     pl.semaphore_wait(barrier, peers)

time: 59.4 us -> 58.8 us (0.990)
  Pallas kernels: 58.5 us -> 57.9 us
    pallas_call x1, Pallas kernels: 53.1 us -> 52.4 us  [moments(): pl.pallas_call(functools.partial(moments_kernel, shape, pairs), out_shape...]
where the time goes in v4:
time: 58.8 us; the launch traced here: 58.7 us
  Pallas kernels  57.9 us (98%)
  between operations  0.8 us (1%)
    pallas_call x1, Pallas kernels, moments(): pl.pallas_call(functools.partial(moments_kernel, shape, pairs), out_shape...  52.4 us
    pallas_call x1, Pallas kernels, project(): pl.pallas_call(functools.partial(project_kernel, tms), out_shape=(out, ou...  5.43 us

profile of v4, /device:TPU:1, one launch (start us, length us, event | category | flops | bytes accessed | tf_op | source)
XLA Modules:
  0.0 58.7 jit_solution(13929667196222666650)
XLA Ops:
  0.6 52.4 %moments.1 = (bf16[5120,256]{1,0:T(8,128)(2,1)}, bf16[2,256,512]{2,1,0:T(8,128)(2,1)}, f32[8,512]{1,0:T(8,128)}) custom-call(bf16[4096,512]{1,0:T(8,128)(2,1)} %bitcast.4, bf16[2,512,512]{2,1,0:T(8,128)(2,1)} %w1_in.1, f32[1,512]{1,0:T(1,128)} %bitcast.5, bf16[2,512,256]{2,1,0:T(8,128)(2,1)} %w2_in.1), custom_call_target="tpu_custom_call" | custom-call | tf_op jit(solution)/shard_map/moments/pallas_call | solution.py:403
  53.1 5.4 %project.1 = (f32[4096,256]{1,0:T(8,128)}, f32[4096,256]{1,0:T(8,128)}) custom-call(bf16[2,256,512]{2,1,0:T(8,128)(2,1)} %get-tuple-element.7.w_in, f32[8,512]{1,0:T(8,128)} %get-tuple-element.8.offs_in, bf16[5120,256]{1,0:T(8,128)(2,1)} %get-tuple-element.9.f_in), custom_call_target="tpu_custom_call" | custom-call | tf_op jit(solution)/shard_map/project/pallas_call | solution.py:526
